TPU v7x, 32 devices: a whole 2x2x4 slice. The times are simulated.
32 devices in a mesh: groups: 2 (over x), frame: 16 (over z, y, core).
Axes of the slice: x: 2, y: 2, z: 4, core: 2. Of those that a mesh axis runs over, the one named last changes fastest.
Arguments:
- queries: bfloat16 [4096, 2048], P(('groups', 'frame')), parts along dimension 0, may hold values from -40 to 40, as said below
- key_rows: bfloat16 [4096, 2048], P(('groups', 'frame')), parts along dimension 0, may hold values from -4 to 4
- value_rows: bfloat16 [4096, 2048], P(('groups', 'frame')), parts along dimension 0, may hold values from -6 to 6
- slopes: bfloat16 [16], replicated, may hold values from 0.0019989014 to 0.19921875
- noise_level: int32 [32], P('groups'), parts along dimension 0, may hold values from 0 to 999
- frame_times: int32 [32], P('groups'), parts along dimension 0, may hold values from 0 to 30, as said below
Outputs:
- advanced: bfloat16 [4096, 2048], P(('groups', 'frame')), parts along dimension 0
There are 2 independent parts, one for each index of `groups`. A program takes and returns all parts, laid end to end along the dimension named above; an argument that names none is the same for every part. Nothing has to cross between parts.
Inputs may be any that keep to these rules, and one draw needn't show every extreme that they name: Rows of queries may be large multiples of key rows. `frame_times`: strictly increasing along the window, starting at 0; neighbouring frames differ by 1 to 3; the last frame stands at 30.
All inputs are finite; a program needn't handle non-finite values.
Results may differ from a plain program's by a relative error of at most 0.009.
Values may be sent and summed in bfloat16 or wider, within the bound.
No kernel may reach another device: no remote copies, remote signals or barrier semaphores. Data moves between devices by JAX's collectives and lax.ppermute only.
A program may use at most 64 MiB of HBM per device.

v0:
```python
import math

import jax
import jax.numpy as jnp
from jax import lax
from jax.sharding import PartitionSpec as P

LEVELS = 1000


def shifted(value, axis, steps):
    count = lax.axis_size(axis)
    first, last = (max(0, -steps), min(count, count - steps))
    return lax.ppermute(value, axis, [(source, source + steps) for source in range(first, last)])


def noise_gates(noise_level):
    phase = (noise_level.astype(jnp.float32) / LEVELS + 0.008) / 1.008
    cosine = jnp.cos(phase * (math.pi / 2))
    signal = cosine * cosine
    return (jnp.sqrt(signal), jnp.sqrt(1.0 - signal))


def spatial_branch(queries, key_rows, value_rows, head_count, head_dim):
    frame_rows = queries.shape[0]
    query_heads = queries.reshape(frame_rows, head_count, head_dim)
    key_heads = key_rows.reshape(frame_rows, head_count, head_dim)
    value_heads = value_rows.reshape(frame_rows, head_count, head_dim)
    scores = jnp.einsum(
        "qhd,khd->hqk", query_heads, key_heads, preferred_element_type=jnp.float32
    ) / math.sqrt(head_dim)
    weights = jax.nn.softmax(scores, axis=-1).astype(jnp.bfloat16)
    attended = jnp.einsum("hqk,khd->qhd", weights, value_heads, preferred_element_type=jnp.float32)
    return attended.reshape(frame_rows, head_count * head_dim)


def temporal_core(query_moved, key_moved, value_moved, slope_vals, distance, noise_gate, head_dim):
    scores = jnp.einsum(
        "qnhd,knhd->nhqk", query_moved, key_moved, preferred_element_type=jnp.float32
    ) / math.sqrt(head_dim)
    penalty = -slope_vals[:, None, None] * distance[None]
    scores = scores + penalty[None]
    weights = jax.nn.softmax(scores, axis=-1).astype(jnp.bfloat16)
    attended = jnp.einsum(
        "nhqk,knhd->qnhd", weights, value_moved, preferred_element_type=jnp.float32
    )
    return (attended * noise_gate[:, None, None, None]).astype(jnp.bfloat16)


def body(queries, key_rows, value_rows, slopes, noise_level, frame_times):
    frame_rows, model_width = queries.shape
    head_count = slopes.shape[0]
    head_dim = model_width // head_count
    signal_gate, noise_gate = noise_gates(noise_level)
    distance = jnp.abs(frame_times[:, None] - frame_times[None, :]).astype(jnp.float32)
    own_gate = lax.dynamic_index_in_dim(signal_gate, lax.axis_index("frame"), 0, keepdims=False)
    query_block = queries.reshape(1, frame_rows, head_count, head_dim)
    key_block = key_rows.reshape(1, frame_rows, head_count, head_dim)
    value_block = value_rows.reshape(1, frame_rows, head_count, head_dim)
    moved_query, moved_key, moved_value = (
        lax.all_to_all(query_block, "frame", split_axis=1, concat_axis=0, tiled=True),
        lax.all_to_all(key_block, "frame", split_axis=1, concat_axis=0, tiled=True),
        lax.all_to_all(value_block, "frame", split_axis=1, concat_axis=0, tiled=True),
    )
    temporal = temporal_core(
        moved_query,
        moved_key,
        moved_value,
        slopes.astype(jnp.float32),
        distance,
        noise_gate,
        head_dim,
    )
    returned = lax.all_to_all(
        jnp.concatenate([temporal[1:], jnp.zeros_like(temporal[:1])], axis=0),
        "frame",
        split_axis=0,
        concat_axis=1,
        tiled=True,
    )
    temporal_rows = returned.reshape(frame_rows, model_width).astype(jnp.float32)
    spatial = spatial_branch(queries, key_rows, value_rows, head_count, head_dim)
    carried = shifted((own_gate * spatial).astype(jnp.bfloat16), "frame", -1).astype(jnp.float32)
    advanced = (carried + temporal_rows).astype(jnp.bfloat16)
    return advanced


def solution(mesh):
    return jax.shard_map(
        body,
        mesh=mesh,
        in_specs=(
            P(("groups", "frame"), None),
            P(("groups", "frame"), None),
            P(("groups", "frame"), None),
            P(),
            P("groups"),
            P("groups"),
        ),
        out_specs=P(("groups", "frame"), None),
        check_vma=False,
    )
```

profile of v0, /device:TPU:13, one launch (start us, length us, event | category | flops | bytes accessed | tf_op | source)
XLA Modules:
  0.0 87.6 jit_solution(10010185706619340784)
XLA Ops:
  0.0 1.9 %copy.39 = bf16[16,8,16,128]{3,2,1,0:T(8,128)(2,1)} copy(bf16[16,8,16,128]{3,1,2,0:T(8,128)(2,1)} %bitcast.63) | data formatting | bytes 1048576
  1.9 6.7 %all-to-all-start = ((bf16[1,128,16,128]{3,2,0,1:T(8,128)(2,1)}), bf16[1,128,16,128]{3,2,0,1:T(8,128)(2,1)S(1)}, u32[]{:S(2)}, u32[]{:S(2)}) async-start(bf16[1,128,16,128]{3,2,0,1:T(8,128)(2,1)} %bitcast.16), calls=%async_computation | async-start | bytes 1048576 | tf_op jit(solution)/shard_map/all_to_all | solution.py:61
  8.6 0.9 %copy.40 = bf16[16,8,16,128]{3,2,1,0:T(8,128)(2,1)} copy(bf16[16,8,16,128]{3,1,2,0:T(8,128)(2,1)S(1)} %bitcast.62) | data formatting | bytes 1048576
  9.5 12.7 %all-to-all-done = bf16[1,128,16,128]{3,2,0,1:T(8,128)(2,1)S(1)} async-done(((bf16[1,128,16,128]{3,2,0,1:T(8,128)(2,1)}), bf16[1,128,16,128]{3,2,0,1:T(8,128)(2,1)S(1)}, u32[]{:S(2)}, u32[]{:S(2)}) %all-to-all-start) | async-done | bytes 524320 | tf_op jit(solution)/shard_map/all_to_all | solution.py:61
  22.2 5.0 %all-to-all-start.1 = ((bf16[1,128,16,128]{3,2,0,1:T(8,128)(2,1)}), bf16[1,128,16,128]{3,2,0,1:T(8,128)(2,1)S(1)}, u32[]{:S(2)}, u32[]{:S(2)}) async-start(bf16[1,128,16,128]{3,2,0,1:T(8,128)(2,1)} %bitcast.20), calls=%async_computation.1 | async-start | bytes 1048576 | tf_op jit(solution)/shard_map/all_to_all | solution.py:62
  27.2 0.9 %copy.41 = bf16[16,8,16,128]{3,2,1,0:T(8,128)(2,1)} copy(bf16[16,8,16,128]{3,1,2,0:T(8,128)(2,1)S(1)} %bitcast.61) | data formatting | bytes 1048576
  28.1 12.7 %all-to-all-done.1 = bf16[1,128,16,128]{3,2,0,1:T(8,128)(2,1)S(1)} async-done(((bf16[1,128,16,128]{3,2,0,1:T(8,128)(2,1)}), bf16[1,128,16,128]{3,2,0,1:T(8,128)(2,1)S(1)}, u32[]{:S(2)}, u32[]{:S(2)}) %all-to-all-start.1) | async-done | bytes 524320 | tf_op jit(solution)/shard_map/all_to_all | solution.py:62
  40.8 5.0 %all-to-all-start.2 = ((bf16[1,128,16,128]{3,2,0,1:T(8,128)(2,1)}), bf16[1,128,16,128]{3,2,0,1:T(8,128)(2,1)S(1)}, u32[]{:S(2)}, u32[]{:S(2)}) async-start(bf16[1,128,16,128]{3,2,0,1:T(8,128)(2,1)} %bitcast.24), calls=%async_computation.2 | async-start | bytes 1048576 | tf_op jit(solution)/shard_map/all_to_all | solution.py:63
  45.8 0.0 copy-done.4
  45.8 0.1 fusion.26
  45.8 0.3 copy.35
  46.1 0.0 copy-start.5
  46.1 0.7 dynamic_slice.4
  46.8 0.6 copy-done.3
  47.4 0.1 abs_convert_fusion
  47.5 0.1 broadcast_multiply_fusion
  47.6 2.0 %fusion.27 = (f32[8,16,16]{2,1,0:T(8,128)S(1)}, f32[8,16,16,16]{2,3,1,0:T(8,128)}) fusion(bf16[16,8,16,128]{3,2,1,0:T(8,128)(2,1)S(1)} %bitcast.66, bf16[16,8,16,128]{3,2,1,0:T(8,128)(2,1)S(1)} %bitcast.64, f32[16,16,16]{1,2,0:T(8,128)S(1)} %broadcast_multiply_fusion), kind=kOutput, calls=%fused_computation.36 | convolution fusion | flops 8519695 | bytes 1204224 | tf_op jit(solution)/shard_map/sub | solution.py:43
  49.6 9.7 %all-to-all-done.2 = bf16[1,128,16,128]{3,2,0,1:T(8,128)(2,1)S(1)} async-done(((bf16[1,128,16,128]{3,2,0,1:T(8,128)(2,1)}), bf16[1,128,16,128]{3,2,0,1:T(8,128)(2,1)S(1)}, u32[]{:S(2)}, u32[]{:S(2)}) %all-to-all-start.2) | async-done | bytes 524320 | tf_op jit(solution)/shard_map/all_to_all | solution.py:63
  59.3 1.7 %fusion.9 = bf16[16,8,16,128]{3,0,2,1:T(8,128)(2,1)S(1)} fusion(f32[8,16,16,16]{2,3,1,0:T(8,128)} %get-tuple-element.8, bf16[16,8,16,128]{3,2,1,0:T(8,128)(2,1)S(1)} %bitcast.67, f32[16]{0:T(128)S(1)} %get-tuple-element.6, f32[8,16,16]{2,1,0:T(8,128)S(1)} %get-tuple-element.7), kind=kOutput, calls=%fused_computation.13 | convolution fusion | flops 8978432 | bytes 1187904 | tf_op jit(solution)/shard_map/nhqk,knhd->qnhd/dot_general | solution.py:44
  61.1 0.2 slice.4
  61.3 0.1 copy.36
  61.4 0.9 concatenate.3.clone
  62.3 5.0 %all-to-all-start.3 = ((bf16[16,8,16,128]{3,2,1,0:T(8,128)(2,1)}), bf16[16,8,16,128]{3,2,1,0:T(8,128)(2,1)S(1)}, u32[]{:S(2)}, u32[]{:S(2)}) async-start(bf16[16,8,16,128]{3,2,1,0:T(8,128)(2,1)} %concatenate.3.clone), calls=%async_computation.3 | async-start | bytes 1048576 | tf_op jit(solution)/shard_map/all_to_all | solution.py:74
  67.3 0.6 fusion.28
  67.8 0.5 convolution_multiply_fusion.3
  68.3 1.1 %fusion.8 = bf16[16,128,128]{1,2,0:T(8,128)(2,1)S(1)} fusion(bf16[128,16,128]{0,2,1:T(8,128)(2,1)S(1)} %bitcast.65, f32[16,128]{1,0:T(8,128)S(1)} %fusion.28, f32[]{:T(128)} %bitcast, f32[16,128,128]{1,2,0:T(8,128)S(1)} %convolution_multiply_fusion.3), kind=kOutput, calls=%fused_computation.12 | convolution fusion | flops 68421760 | bytes 2105348 | tf_op jit(solution)/shard_map/hqk,khd->qhd/dot_general | solution.py:33
  69.4 0.2 copy.27
  69.6 2.3 %collective-permute-start = (bf16[128,2048]{1,0:T(8,128)(2,1)S(1)}, bf16[128,2048]{1,0:T(8,128)(2,1)S(1)}, u32[]{:S(2)}, u32[]{:S(2)}) collective-permute-start(bf16[128,2048]{1,0:T(8,128)(2,1)S(1)} %copy.27), channel_id=1, source_target_pairs={{1,0},{2,1},{3,2},{4,3},{5,4},{6,5},{7,6},{8,7},{9,8},{10,9},{11,1... | collective-permute-start | bytes 1572872 | tf_op jit(solution)/shard_map/ppermute | solution.py:14
  71.9 8.9 %all-to-all-done.3 = bf16[16,8,16,128]{3,2,1,0:T(8,128)(2,1)S(1)} async-done(((bf16[16,8,16,128]{3,2,1,0:T(8,128)(2,1)}), bf16[16,8,16,128]{3,2,1,0:T(8,128)(2,1)S(1)}, u32[]{:S(2)}, u32[]{:S(2)}) %all-to-all-start.3) | async-done | bytes 524320 | tf_op jit(solution)/shard_map/all_to_all | solution.py:74
  80.9 0.1 convert_bitcast_fusion
  81.0 5.5 %collective-permute-done = bf16[128,2048]{1,0:T(8,128)(2,1)S(1)} collective-permute-done((bf16[128,2048]{1,0:T(8,128)(2,1)S(1)}, bf16[128,2048]{1,0:T(8,128)(2,1)S(1)}, u32[]{:S(2)}, u32[]{:S(2)}) %collective-permute-start) | collective-permute-done | bytes 524320 | tf_op jit(solution)/shard_map/ppermute | solution.py:14
  86.5 1.1 %fusion.10 = bf16[128,2048]{1,0:T(8,128)(2,1)} fusion(f32[16,8,16,128]{3,2,1,0:T(8,128)S(1)} %convert_bitcast_fusion, bf16[128,2048]{1,0:T(8,128)(2,1)S(1)} %collective-permute-done), kind=kLoop, calls=%fused_computation.15 | loop fusion | flops 786432 | bytes 2097152 | tf_op jit(solution)/shard_map/convert_element_type | solution.py:84
  (10 shorter events, 0.0 us)
Async XLA Ops:
  1.9 6.7 %copy-start.1 = (bf16[128,2048]{1,0:T(8,128)(2,1)S(1)}, bf16[128,2048]{1,0:T(8,128)(2,1)}, u32[]{:S(2)}) copy-start(bf16[128,2048]{1,0:T(8,128)(2,1)} %param.7) | copy-start | bytes 1572868
  1.9 20.2 %all-to-all-start = ((bf16[1,128,16,128]{3,2,0,1:T(8,128)(2,1)}), bf16[1,128,16,128]{3,2,0,1:T(8,128)(2,1)S(1)}, u32[]{:S(2)}, u32[]{:S(2)}) async-start(bf16[1,128,16,128]{3,2,0,1:T(8,128)(2,1)} %bitcast.16), calls=%async_computation | async-start | bytes 1048576 | tf_op jit(solution)/shard_map/all_to_all | solution.py:61
  22.2 5.0 %copy-start = (bf16[128,2048]{1,0:T(8,128)(2,1)S(1)}, bf16[128,2048]{1,0:T(8,128)(2,1)}, u32[]{:S(2)}) copy-start(bf16[128,2048]{1,0:T(8,128)(2,1)} %param.8) | copy-start | bytes 1572868
  22.2 18.6 %all-to-all-start.1 = ((bf16[1,128,16,128]{3,2,0,1:T(8,128)(2,1)}), bf16[1,128,16,128]{3,2,0,1:T(8,128)(2,1)S(1)}, u32[]{:S(2)}, u32[]{:S(2)}) async-start(bf16[1,128,16,128]{3,2,0,1:T(8,128)(2,1)} %bitcast.20), calls=%async_computation.1 | async-start | bytes 1048576 | tf_op jit(solution)/shard_map/all_to_all | solution.py:62
  40.8 5.0 %copy-start.4 = (s32[16]{0:T(128)S(1)}, s32[16]{0:T(128)}, u32[]{:S(2)}) copy-start(s32[16]{0:T(128)} %param.10) | copy-start | bytes 196
  40.8 18.6 %all-to-all-start.2 = ((bf16[1,128,16,128]{3,2,0,1:T(8,128)(2,1)}), bf16[1,128,16,128]{3,2,0,1:T(8,128)(2,1)S(1)}, u32[]{:S(2)}, u32[]{:S(2)}) async-start(bf16[1,128,16,128]{3,2,0,1:T(8,128)(2,1)} %bitcast.24), calls=%async_computation.2 | async-start | bytes 1048576 | tf_op jit(solution)/shard_map/all_to_all | solution.py:63
  46.1 0.7 copy-start.5
  46.8 0.7 copy-start.3
  62.3 5.0 %copy-start.2 = (bf16[128,2048]{1,0:T(8,128)(2,1)S(1)}, bf16[128,2048]{1,0:T(8,128)(2,1)}, u32[]{:S(2)}) copy-start(bf16[128,2048]{1,0:T(8,128)(2,1)} %param.6) | copy-start | bytes 1572868
  62.3 18.6 %all-to-all-start.3 = ((bf16[16,8,16,128]{3,2,1,0:T(8,128)(2,1)}), bf16[16,8,16,128]{3,2,1,0:T(8,128)(2,1)S(1)}, u32[]{:S(2)}, u32[]{:S(2)}) async-start(bf16[16,8,16,128]{3,2,1,0:T(8,128)(2,1)} %concatenate.3.clone), calls=%async_computation.3 | async-start | bytes 1048576 | tf_op jit(solution)/shard_map/all_to_all | solution.py:74
  69.6 16.9 %collective-permute-start = (bf16[128,2048]{1,0:T(8,128)(2,1)S(1)}, bf16[128,2048]{1,0:T(8,128)(2,1)S(1)}, u32[]{:S(2)}, u32[]{:S(2)}) collective-permute-start(bf16[128,2048]{1,0:T(8,128)(2,1)S(1)} %copy.27), channel_id=1, source_target_pairs={{1,0},{2,1},{3,2},{4,3},{5,4},{6,5},{7,6},{8,7},{9,8},{10,9},{11,1... | collective-permute-start | bytes 1572872 | tf_op jit(solution)/shard_map/ppermute | solution.py:14
where the time goes:
time: 88.3 us; the launch traced here: 87.6 us
  waiting for transfers between devices  49.5 us (56%)
  starting transfers between devices  24 us (27%)
  local copies, waits for them, and re-layouts  6.76 us (8%)
  matrix products  5.84 us (7%)
  other arithmetic  1.45 us (2%)
    all_to_all x1, waiting for transfers between devices, body(): lax.all_to_all(query_block, 'frame', split_axis=1, concat_axis=0, tiled=T...  12.7 us
    all_to_all x1, waiting for transfers between devices, body(): lax.all_to_all(key_block, 'frame', split_axis=1, concat_axis=0, tiled=True)  12.7 us
    all_to_all x1, waiting for transfers between devices, body(): lax.all_to_all(value_block, 'frame', split_axis=1, concat_axis=0, tiled=T...  9.72 us
    all_to_all x1, waiting for transfers between devices, body(): lax.all_to_all(jnp.concatenate([temporal[1:], jnp.zeros_like(temporal[:1]...  8.93 us
    all_to_all x1, starting transfers between devices, body(): lax.all_to_all(query_block, 'frame', split_axis=1, concat_axis=0, tiled=T...  6.65 us
    ppermute x1, waiting for transfers between devices, shifted(): lax.ppermute(value, axis, [(source, source + steps) for source in range(f...  5.5 us
    all_to_all x1, starting transfers between devices, body(): lax.all_to_all(key_block, 'frame', split_axis=1, concat_axis=0, tiled=True)  5 us
    all_to_all x1, starting transfers between devices, body(): lax.all_to_all(value_block, 'frame', split_axis=1, concat_axis=0, tiled=T...  5 us
  transfers between devices with their start and end apart: 5, of which 5 were waited for; matrix products, arithmetic and copies ran while one was open for 8% of the time, Pallas kernels for 0%

commit v1 on v0

v1 whole, which is shorter than its diff:
```python
import functools
import math

import jax
import jax.numpy as jnp
from jax import lax
from jax.experimental import pallas as pl
from jax.experimental.pallas import tpu as pltpu
from jax.sharding import PartitionSpec as P

LEVELS = 1000
FAR = 1e30
VMEM_BYTES = 24 << 20


def shifted(value, axis, steps):
    count = lax.axis_size(axis)
    first, last = (max(0, -steps), min(count, count - steps))
    return lax.ppermute(value, axis, [(source, source + steps) for source in range(first, last)])


def noise_gates(noise_level):
    phase = (noise_level.astype(jnp.float32) / LEVELS + 0.008) / 1.008
    cosine = jnp.cos(phase * (math.pi / 2))
    signal = cosine * cosine
    return (jnp.sqrt(signal), jnp.sqrt(1.0 - signal))


def head_attention(query, key, value, scale, penalty):
    scores = lax.dot_general(query, key, (((1,), (1,)), ((), ())), preferred_element_type=jnp.float32) * scale
    if penalty is not None:
        scores = scores - penalty
    peak = jnp.max(scores, axis=-1, keepdims=True)
    raised = jnp.exp(scores - peak)
    weights = (raised * (1.0 / jnp.sum(raised, axis=-1, keepdims=True))).astype(jnp.bfloat16)
    return jnp.dot(weights, value, preferred_element_type=jnp.float32)


def temporal_kernel(head_dim, share, slopes_ref, moved_ref, distance_ref, gate_ref, out_ref):
    rows, width = out_ref.shape
    distance = distance_ref[...]
    gate = gate_ref[...]
    kept = lax.broadcasted_iota(jnp.int32, (rows, head_dim), 0) < rows - share
    for head in range(width // head_dim):
        spans = [pl.ds(part * width + head * head_dim, head_dim) for part in range(3)]
        attended = head_attention(
            moved_ref[:, spans[0]],
            moved_ref[:, spans[1]],
            moved_ref[:, spans[2]],
            1.0 / math.sqrt(head_dim),
            slopes_ref[head] * distance,
        )
        earlier = pltpu.roll(attended * gate, rows - share, 0)
        out_ref[:, spans[0]] = jnp.where(kept, earlier, 0.0).astype(out_ref.dtype)


def spatial_kernel(head_dim, gate_ref, query_ref, key_ref, value_ref, out_ref):
    rows, width = out_ref.shape
    gate = gate_ref[0]
    for head in range(width // head_dim):
        span = pl.ds(head * head_dim, head_dim)
        attended = head_attention(
            query_ref[:, span], key_ref[:, span], value_ref[:, span], 1.0 / math.sqrt(head_dim), None
        )
        out_ref[:, span] = (attended * gate).astype(out_ref.dtype)


def cost(rows, width, operands):
    return pl.CostEstimate(
        flops=4 * rows * rows * width, bytes_accessed=operands * 2 * rows * width, transcendentals=rows * rows * 16
    )


def body(queries, key_rows, value_rows, slopes, noise_level, frame_times):
    frame_rows, model_width = queries.shape
    head_count = slopes.shape[0]
    head_dim = model_width // head_count
    count = lax.axis_size("frame")
    share = frame_rows // count
    vmem = pl.BlockSpec(memory_space=pltpu.VMEM)
    smem = pl.BlockSpec(memory_space=pltpu.SMEM)
    signal_gate, noise_gate = noise_gates(noise_level)
    own_gate = lax.dynamic_slice_in_dim(signal_gate, lax.axis_index("frame"), 1)

    moved = lax.all_to_all(
        jnp.concatenate([queries, key_rows, value_rows], axis=1), "frame", split_axis=0, concat_axis=0, tiled=True
    )

    spatial = pl.pallas_call(
        functools.partial(spatial_kernel, head_dim),
        out_shape=jax.ShapeDtypeStruct((frame_rows, model_width), jnp.bfloat16),
        in_specs=[smem, vmem, vmem, vmem],
        out_specs=vmem,
        cost_estimate=cost(frame_rows, model_width, 4),
        compiler_params=pltpu.CompilerParams(vmem_limit_bytes=VMEM_BYTES),
        name="spatial",
    )(own_gate, queries, key_rows, value_rows)
    carried = shifted(spatial, "frame", -1)

    rows = count * share
    row_times = jnp.repeat(frame_times.astype(jnp.float32), share)
    row_tokens = lax.rem(jnp.arange(rows), share)
    distance = jnp.where(
        row_tokens[:, None] == row_tokens[None, :], jnp.abs(row_times[:, None] - row_times[None, :]), FAR
    )
    gate_rows = jnp.broadcast_to(jnp.repeat(noise_gate, share)[:, None], (rows, head_dim))
    temporal = pl.pallas_call(
        functools.partial(temporal_kernel, head_dim, share),
        out_shape=jax.ShapeDtypeStruct((rows, model_width), jnp.bfloat16),
        in_specs=[smem, vmem, vmem, vmem],
        out_specs=vmem,
        cost_estimate=cost(rows, model_width, 4),
        compiler_params=pltpu.CompilerParams(vmem_limit_bytes=VMEM_BYTES),
        name="temporal",
    )(slopes.astype(jnp.float32), moved, distance, gate_rows)
    returned = lax.all_to_all(temporal, "frame", split_axis=0, concat_axis=0, tiled=True)
    return (carried.astype(jnp.float32) + returned.astype(jnp.float32)).astype(jnp.bfloat16)


def solution(mesh):
    return jax.shard_map(
        body,
        mesh=mesh,
        in_specs=(
            P(("groups", "frame"), None),
            P(("groups", "frame"), None),
            P(("groups", "frame"), None),
            P(),
            P("groups"),
            P("groups"),
        ),
        out_specs=P(("groups", "frame"), None),
        check_vma=False,
    )
```

time: 88.3 us -> 77.4 us (0.88)
  Pallas kernels: 0 us -> 12.4 us
  starting transfers between devices: 24 us -> 13.7 us
  matrix products: 5.84 us -> 0 us
  local copies, waits for them, and re-layouts: 6.76 us -> 1.07 us
  waiting for transfers between devices: 49.5 us -> 46 us
  other arithmetic: 1.45 us -> 3.73 us
    pallas_call x0 -> x2, Pallas kernels: none -> 12.4 us  [the longest x1 6.59 us: body(): pl.pallas_call(functools.partial(temporal_kernel, head_dim, share), out_s...]
    all_to_all x4 -> x2, starting transfers between devices: 21.7 us -> 11.4 us  [the longest x1 6.65 us: body(): lax.all_to_all(jnp.concatenate([queries, key_rows, value_rows], axis=1),...]
    all_to_all x4 -> x2, waiting for transfers between devices: 44 us -> 35.6 us  [the longest x1 35.6 us: body(): lax.all_to_all(jnp.concatenate([queries, key_rows, value_rows], axis=1),...]
    ppermute x1, waiting for transfers between devices: 5.5 us -> 10.4 us  [shifted(): lax.ppermute(value, axis, [(source, source + steps) for source in range(f...]
    unnamed x16 -> x12, local copies, waits for them, and re-layouts: 4.56 us -> 0.03 us
    dot_general x3 -> x0, matrix products: 3.27 us -> none  [the longest x1 1.74 us: temporal_core(): jnp.einsum('nhqk,knhd->qnhd', weights, value_moved, preferred_element_typ...]
    all_to_all x0 -> x1, other arithmetic: none -> 2.65 us  [body(): lax.all_to_all(jnp.concatenate([queries, key_rows, value_rows], axis=1),...]
    sub x2 -> x0, matrix products: 2.57 us -> none  [the longest x1 2.02 us: temporal_core(): weights = jax.nn.softmax(scores, axis=-1).astype(jnp.bfloat16)]
  transfers between devices with their start and end apart: 5 -> 3, of which waited for: 5 -> 2; matrix products, arithmetic and copies ran while one was open for 8% -> 1% of each run, Pallas kernels for 0% -> 8%
where the time goes in v1:
time: 77.4 us; the launch traced here: 77.1 us
  waiting for transfers between devices  46 us (59%)
  starting transfers between devices  13.7 us (18%)
  Pallas kernels  12.4 us (16%)
  other arithmetic  3.73 us (5%)
  local copies, waits for them, and re-layouts  1.07 us (1%)
    all_to_all x1, waiting for transfers between devices, body(): lax.all_to_all(jnp.concatenate([queries, key_rows, value_rows], axis=1),...  35.6 us
    ppermute x1, waiting for transfers between devices, shifted(): lax.ppermute(value, axis, [(source, source + steps) for source in range(f...  10.4 us
    all_to_all x1, starting transfers between devices, body(): lax.all_to_all(jnp.concatenate([queries, key_rows, value_rows], axis=1),...  6.65 us
    pallas_call x1, Pallas kernels, body(): pl.pallas_call(functools.partial(temporal_kernel, head_dim, share), out_s...  6.59 us
    pallas_call x1, Pallas kernels, body(): pl.pallas_call(functools.partial(spatial_kernel, head_dim), out_shape=jax...  5.85 us
    all_to_all x1, starting transfers between devices, body(): lax.all_to_all(temporal, 'frame', split_axis=0, concat_axis=0, tiled=True)  4.78 us
    all_to_all x1, other arithmetic, body(): lax.all_to_all(jnp.concatenate([queries, key_rows, value_rows], axis=1),...  2.65 us
    ppermute x1, starting transfers between devices, shifted(): lax.ppermute(value, axis, [(source, source + steps) for source in range(f...  2.3 us
  transfers between devices with their start and end apart: 3, of which 2 were waited for; matrix products, arithmetic and copies ran while one was open for 1% of the time, Pallas kernels for 8%

profile of v1, /device:TPU:13, one launch (start us, length us, event | category | flops | bytes accessed | tf_op | source)
XLA Modules:
  0.0 77.1 jit_solution(2524279767564622039)
XLA Ops:
  0.0 2.6 %maximum_bitcast_fusion = bf16[16,8,6144]{2,1,0:T(8,128)(2,1)} fusion(bf16[128,2048]{1,0:T(8,128)(2,1)} %value_ref.1, bf16[128,2048]{1,0:T(8,128)(2,1)} %key_ref.1, bf16[128,2048]{1,0:T(8,128)(2,1)} %query_ref.1), kind=kLoop, calls=%fused_computation | loop fusion | flops 4718592 | bytes 3145728 | tf_op jit(solution)/shard_map/all_to_all | solution.py:85
  2.6 0.0 copy-start.3
  2.7 0.0 copy-start.4
  2.7 0.0 copy-start.5
  2.7 6.7 %all-to-all-start = ((bf16[16,8,6144]{2,1,0:T(8,128)(2,1)}), bf16[16,8,6144]{2,1,0:T(8,128)(2,1)S(1)}, u32[]{:S(2)}, u32[]{:S(2)}) async-start(bf16[16,8,6144]{2,1,0:T(8,128)(2,1)} %maximum_bitcast_fusion), calls=%async_computation | async-start | bytes 3145728 | tf_op jit(solution)/shard_map/all_to_all | solution.py:85
  9.3 0.0 copy-done.3
  9.3 0.0 copy-done.4
  9.3 0.1 broadcast_in_dim.19
  9.4 0.1 sub.18
  9.5 0.0 copy-done.5
  9.5 0.1 subtract_sqrt_fusion
  9.6 0.1 broadcast_in_dim.21
  9.6 0.1 broadcast_in_dim.22
  9.8 0.1 abs_select_fusion.distance_ref
  9.9 35.6 %all-to-all-done = bf16[16,8,6144]{2,1,0:T(8,128)(2,1)S(1)} async-done(((bf16[16,8,6144]{2,1,0:T(8,128)(2,1)}), bf16[16,8,6144]{2,1,0:T(8,128)(2,1)S(1)}, u32[]{:S(2)}, u32[]{:S(2)}) %all-to-all-start) | async-done | bytes 1572896 | tf_op jit(solution)/shard_map/all_to_all | solution.py:85
  45.5 0.1 broadcast_in_dim.23.gate_ref
  45.6 0.0 copy-start
  45.6 0.0 copy-start.1
  45.6 0.0 copy-start.2
  45.6 6.6 %temporal.1 = bf16[128,2048]{1,0:T(8,128)(2,1)} custom-call(f32[16]{0:T(128)S(1)} %convert_element_type.23.slopes_ref, bf16[128,6144]{1,0:T(8,128)(2,1)S(1)} %bitcast.7, f32[128,128]{1,0:T(8,128)S(1)} %abs_select_fusion.distance_ref, f32[128,128]{1,0:T(8,128)S(1)} %broadcast_in_dim.23.gate_ref), custom_call_target="tpu_custom_call" | custom-call | flops 134217728 | bytes 2097152 | tf_op jit(solution)/shard_map/temporal/pallas_call | solution.py:107
  52.2 4.8 %all-to-all-start.1 = ((bf16[16,8,2048]{2,1,0:T(8,128)(2,1)}), bf16[16,8,2048]{2,1,0:T(8,128)(2,1)S(1)}, u32[]{:S(2)}, u32[]{:S(2)}) async-start(bf16[16,8,2048]{2,1,0:T(8,128)(2,1)} %bitcast.2), calls=%async_computation.1 | async-start | bytes 1048576 | tf_op jit(solution)/shard_map/all_to_all | solution.py:116
  57.0 0.6 dynamic_slice.3.gate_ref
  57.6 0.0 copy-done
  57.6 0.0 copy-done.1
  57.6 0.0 copy-done.2
  57.6 5.8 %spatial.1 = bf16[128,2048]{1,0:T(8,128)(2,1)S(1)} custom-call(f32[1]{0:T(128)} %dynamic_slice.3.gate_ref, bf16[128,2048]{1,0:T(8,128)(2,1)S(1)} %copy-done, bf16[128,2048]{1,0:T(8,128)(2,1)S(1)} %copy-done.1, bf16[128,2048]{1,0:T(8,128)(2,1)S(1)} %copy-done.2), custom_call_target="tpu_custom_call" | custom-call | flops 134217728 | bytes 2097152 | tf_op jit(solution)/shard_map/spatial/pallas_call | solution.py:89
  63.5 2.3 %collective-permute-start = (bf16[128,2048]{1,0:T(8,128)(2,1)S(1)}, bf16[128,2048]{1,0:T(8,128)(2,1)S(1)}, u32[]{:S(2)}, u32[]{:S(2)}) collective-permute-start(bf16[128,2048]{1,0:T(8,128)(2,1)S(1)} %spatial.1), channel_id=1, source_target_pairs={{1,0},{2,1},{3,2},{4,3},{5,4},{6,5},{7,6},{8,7},{9,8},{10,9},{11,1... | collective-permute-start | bytes 1572872 | tf_op jit(solution)/shard_map/ppermute | solution.py:19
  65.8 10.4 %collective-permute-done = bf16[128,2048]{1,0:T(8,128)(2,1)S(1)} collective-permute-done((bf16[128,2048]{1,0:T(8,128)(2,1)S(1)}, bf16[128,2048]{1,0:T(8,128)(2,1)S(1)}, u32[]{:S(2)}, u32[]{:S(2)}) %collective-permute-start) | collective-permute-done | bytes 524320 | tf_op jit(solution)/shard_map/ppermute | solution.py:19
  76.2 0.0 all-to-all-done.1
  76.2 0.9 %fusion = bf16[128,2048]{1,0:T(8,128)(2,1)} fusion(bf16[128,2048]{1,0:T(8,128)(2,1)S(1)} %collective-permute-done, bf16[16,8,2048]{2,1,0:T(8,128)(2,1)S(1)} %all-to-all-done.1), kind=kLoop, calls=%fused_computation.2 | loop fusion | flops 1048576 | bytes 1572864 | tf_op jit(solution)/shard_map/convert_element_type | solution.py:117
  (3 shorter events, 0.0 us)
Async XLA Ops:
  2.6 6.7 %copy-start.3 = (bf16[16]{0:T(256)(128)(2,1)S(1)}, bf16[16]{0:T(256)(128)(2,1)}, u32[]{:S(2)}) copy-start(bf16[16]{0:T(256)(128)(2,1)} %param.9) | copy-start | bytes 100
  2.7 6.7 %copy-start.4 = (s32[16]{0:T(128)S(1)}, s32[16]{0:T(128)}, u32[]{:S(2)}) copy-start(s32[16]{0:T(128)} %param.11) | copy-start | bytes 196
  2.7 6.9 %copy-start.5 = (s32[16]{0:T(128)S(1)}, s32[16]{0:T(128)}, u32[]{:S(2)}) copy-start(s32[16]{0:T(128)} %param.10) | copy-start | bytes 196
  2.7 42.8 %all-to-all-start = ((bf16[16,8,6144]{2,1,0:T(8,128)(2,1)}), bf16[16,8,6144]{2,1,0:T(8,128)(2,1)S(1)}, u32[]{:S(2)}, u32[]{:S(2)}) async-start(bf16[16,8,6144]{2,1,0:T(8,128)(2,1)} %maximum_bitcast_fusion), calls=%async_computation | async-start | bytes 3145728 | tf_op jit(solution)/shard_map/all_to_all | solution.py:85
  45.6 12.0 %copy-start = (bf16[128,2048]{1,0:T(8,128)(2,1)S(1)}, bf16[128,2048]{1,0:T(8,128)(2,1)}, u32[]{:S(2)}) copy-start(bf16[128,2048]{1,0:T(8,128)(2,1)} %query_ref.1) | copy-start | bytes 1572868
  45.6 12.0 %copy-start.1 = (bf16[128,2048]{1,0:T(8,128)(2,1)S(1)}, bf16[128,2048]{1,0:T(8,128)(2,1)}, u32[]{:S(2)}) copy-start(bf16[128,2048]{1,0:T(8,128)(2,1)} %key_ref.1) | copy-start | bytes 1572868
  45.6 12.0 %copy-start.2 = (bf16[128,2048]{1,0:T(8,128)(2,1)S(1)}, bf16[128,2048]{1,0:T(8,128)(2,1)}, u32[]{:S(2)}) copy-start(bf16[128,2048]{1,0:T(8,128)(2,1)} %value_ref.1) | copy-start | bytes 1572868
  52.2 24.0 %all-to-all-start.1 = ((bf16[16,8,2048]{2,1,0:T(8,128)(2,1)}), bf16[16,8,2048]{2,1,0:T(8,128)(2,1)S(1)}, u32[]{:S(2)}, u32[]{:S(2)}) async-start(bf16[16,8,2048]{2,1,0:T(8,128)(2,1)} %bitcast.2), calls=%async_computation.1 | async-start | bytes 1048576 | tf_op jit(solution)/shard_map/all_to_all | solution.py:116
  63.5 12.7 %collective-permute-start = (bf16[128,2048]{1,0:T(8,128)(2,1)S(1)}, bf16[128,2048]{1,0:T(8,128)(2,1)S(1)}, u32[]{:S(2)}, u32[]{:S(2)}) collective-permute-start(bf16[128,2048]{1,0:T(8,128)(2,1)S(1)} %spatial.1), channel_id=1, source_target_pairs={{1,0},{2,1},{3,2},{4,3},{5,4},{6,5},{7,6},{8,7},{9,8},{10,9},{11,1... | collective-permute-start | bytes 1572872 | tf_op jit(solution)/shard_map/ppermute | solution.py:19
